TPU v7x, 32 devices: a whole 2x2x4 slice. The times are simulated.
32 devices in a mesh: gx: 4 (over y, x), gy: 4 (over z), gz: 2 (over core).
Axes of the slice: x: 2, y: 2, z: 4, core: 2. Of those that a mesh axis runs over, the one named last changes fastest.
Arguments:
- force: float32 [3, 128, 64, 256], P(None, 'gx', 'gy', 'gz'), may hold values from -6 to 6
- phase: int32 [128, 64, 256], P('gx', 'gy', 'gz'), may hold values from 0 to 7
- viscosity_table: float32 [8], replicated, may hold values from 0.1 to 10
- boundary_flags: int32 [6], replicated, may hold values from 0 to 1
Outputs:
- pressure: float32 [128, 64, 256], P('gx', 'gy', 'gz')
- residual: float32 [128, 64, 256], P('gx', 'gy', 'gz')
- res_norms: float32 [3], replicated
Inputs may be any that keep to these rules, and one draw needn't show every extreme that they name: phase ids index viscosity_table. `boundary_flags`: 0 marks a no-slip face, 1 a free-slip face.
All inputs are finite; a program needn't handle non-finite values.
Results may differ from a plain program's by a relative error of at most 0.0003.
Values sent between devices are 32-bit elements; how exact they have to be, the bound alone decides.
A program may use at most 192 MiB of HBM per device.

v0:
```python
import jax
import jax.numpy as jnp
from jax import lax
from jax.sharding import PartitionSpec as P

ITERS = 3
SWEEPS = 4
OMEGA = 0.8


def passed_along(value, axis, by):
    devices = lax.axis_size(axis)
    pairs = [(i, i + by) for i in range(devices) if 0 <= i + by < devices]
    return lax.ppermute(value, axis, pairs)


def extended(cells, sides, width):
    for axis, dim in sides:
        count = lax.axis_size(axis)
        ends = count - 1
        head = lax.slice_in_dim(cells, 0, width, axis=dim)
        tail = lax.slice_in_dim(cells, cells.shape[dim] - width, cells.shape[dim], axis=dim)
        cells = jnp.concatenate(
            [
                lax.ppermute(tail, axis, [(i, (i + 1) % count) for i in range(ends)]),
                cells,
                lax.ppermute(head, axis, [((i + 1) % count, i) for i in range(ends)]),
            ],
            axis=dim,
        )
    return cells


def lookup(phase, table):
    eta = jnp.zeros(phase.shape, jnp.float32)
    for level in range(table.shape[0]):
        eta = eta + jnp.where(phase == level, table[level], jnp.float32(0.0))
    return eta


def trim(array, keep):
    for dim in range(3):
        if dim != keep:
            array = lax.slice_in_dim(array, 1, array.shape[dim] - 1, axis=dim)
    return array


def coefficients(eta_wide, flags, starts, totals):
    walls = (flags == 0).astype(jnp.float32)
    inner = eta_wide[1:-1, 1:-1, 1:-1]
    faces = []
    diag = [jnp.zeros_like(inner) for comp in range(3)]
    for axis in range(3):
        length = eta_wide.shape[axis]
        spots = starts[axis] + jnp.arange(length, dtype=jnp.int32)
        inside = (spots >= 0) & (spots < totals[axis])
        shape = [1, 1, 1]
        shape[axis] = length - 2
        upper_in = inside[2:].reshape(shape)
        lower_in = inside[:-2].reshape(shape)
        sides = trim(eta_wide, axis)
        middle = lax.slice_in_dim(sides, 1, length - 1, axis=axis)
        upper = 0.5 * (middle + lax.slice_in_dim(sides, 2, length, axis=axis))
        lower = 0.5 * (middle + lax.slice_in_dim(sides, 0, length - 2, axis=axis))
        faces.append((jnp.where(upper_in, upper, 0.0), jnp.where(lower_in, lower, 0.0)))
        for comp in range(3):
            normal = 1.0 if comp == axis else 0.0
            wall_low = jnp.maximum(walls[2 * axis], normal)
            wall_high = jnp.maximum(walls[2 * axis + 1], normal)
            diag[comp] = (
                diag[comp]
                + jnp.where(upper_in, upper, wall_high * inner)
                + jnp.where(lower_in, lower, wall_low * inner)
            )
    return (faces, jnp.stack(diag))


def viscous(state, faces, diag):
    ends = []
    for axis, name in enumerate(("gx", "gy", "gz")):
        dim = axis + 1
        length = state.shape[dim]
        head = lax.slice_in_dim(state, 0, 1, axis=dim)
        tail = lax.slice_in_dim(state, length - 1, length, axis=dim)
        ends.append((passed_along(head, name, -1), passed_along(tail, name, 1)))
    result = diag * state
    for axis in range(3):
        dim = axis + 1
        length = state.shape[dim]
        above, below = ends[axis]
        upper = jnp.concatenate([lax.slice_in_dim(state, 1, length, axis=dim), above], dim)
        lower = jnp.concatenate([below, lax.slice_in_dim(state, 0, length - 1, axis=dim)], dim)
        result = result - faces[axis][0] * upper
        result = result - faces[axis][1] * lower
    return result


def gradient(field):
    upper_x = passed_along(field[0:1], "gx", -1)
    upper_y = passed_along(field[:, 0:1], "gy", -1)
    upper_z = passed_along(field[:, :, 0:1], "gz", -1)
    along_x = jnp.concatenate([field[1:], upper_x], 0) - field
    along_y = jnp.concatenate([field[:, 1:], upper_y], 1) - field
    along_z = jnp.concatenate([field[:, :, 1:], upper_z], 2) - field
    return jnp.stack([along_x, along_y, along_z])


def divergence(velocity):
    lower_x = passed_along(velocity[0][-1:], "gx", 1)
    lower_y = passed_along(velocity[1][:, -1:], "gy", 1)
    lower_z = passed_along(velocity[2][:, :, -1:], "gz", 1)
    total = jnp.concatenate([lower_x, velocity[0][:-1]], 0) - velocity[0]
    total = total + jnp.concatenate([lower_y, velocity[1][:, :-1]], 1) - velocity[1]
    total = total + jnp.concatenate([lower_z, velocity[2][:, :, :-1]], 2) - velocity[2]
    return total


def per_device(force, phase, viscosity_table, boundary_flags):
    rows = phase.shape
    totals = (
        rows[0] * lax.axis_size("gx"),
        rows[1] * lax.axis_size("gy"),
        rows[2] * lax.axis_size("gz"),
    )
    indices = (lax.axis_index("gx"), lax.axis_index("gy"), lax.axis_index("gz"))
    cells = float(totals[0] * totals[1] * totals[2])
    phase_wide = extended(phase, (("gx", 0), ("gy", 1), ("gz", 2)), 1)
    starts = tuple((indices[dim] * rows[dim] - 1 for dim in range(3)))
    eta_wide = lookup(phase_wide, viscosity_table)
    faces, diag = coefficients(eta_wide, boundary_flags, starts, totals)
    eta = eta_wide[1:-1, 1:-1, 1:-1]
    inverse = 1.0 / diag

    def sweeps(source, state, count):
        for sweep in range(count):
            state = state + OMEGA * inverse * (source - viscous(state, faces, diag))
        return state

    def schur(field):
        source = gradient(field)
        return divergence(sweeps(source, OMEGA * inverse * source, SWEEPS - 1))

    rhs = divergence(sweeps(force, OMEGA * inverse * force, SWEEPS - 1))
    pressure = jnp.zeros_like(rhs)
    residual = rhs
    norms = []
    scaled = eta * residual
    applied = schur(scaled)
    for step in range(ITERS):
        last = step + 1 == ITERS
        gamma, delta, squares = lax.psum(
            (jnp.sum(residual * scaled), jnp.sum(applied * scaled), jnp.sum(residual * residual)),
            ("gx", "gy", "gz"),
        )
        norms.append(squares / cells)
        if not last:
            mass_applied = eta * applied
            twice_applied = schur(mass_applied)
        if step == 0:
            alpha = gamma / delta
            search = scaled
            search_image = applied
            scaled_image = mass_applied
            applied_image = twice_applied
        else:
            beta = gamma / gamma_old
            alpha = gamma / (delta - beta * gamma / alpha_old)
            search = scaled + beta * search
            search_image = applied + beta * search_image
            if not last:
                scaled_image = mass_applied + beta * scaled_image
                applied_image = twice_applied + beta * applied_image
        pressure = pressure + alpha * search
        residual = residual - alpha * search_image
        if not last:
            scaled = scaled - alpha * scaled_image
            applied = applied - alpha * applied_image
        gamma_old = gamma
        alpha_old = alpha
    return (pressure, residual, jnp.stack(norms))


def solution(mesh):
    placed = (P(None, "gx", "gy", "gz"), P("gx", "gy", "gz"), P(), P())
    return jax.shard_map(
        per_device,
        mesh=mesh,
        in_specs=placed,
        out_specs=(P("gx", "gy", "gz"), P("gx", "gy", "gz"), P()),
        check_vma=False,
    )
```

profile of v0, /device:TPU:0, one launch (start us, length us, event | category | flops | bytes accessed | tf_op | source)
XLA Modules:
  0.0 667.3 jit_solution(11846374254720408442)
XLA Ops:
  2.6 5.5 collective-permute-start
  31.1 6.0 select_add_fusion
  82.9 6.3 collective-permute-start.13
  90.5 4.5 collective-permute-start.15
  118.6 5.5 collective-permute-start.19
  143.0 4.9 collective-permute-start.24
  175.8 5.3 collective-permute-start.31
  182.4 4.5 collective-permute-start.33
  211.6 5.1 collective-permute-start.37
  246.1 5.5 collective-permute-start.43
  270.5 4.9 collective-permute-start.48
  290.0 45.0 %all-reduce.2 = (f32[]{:T(128)}, f32[]{:T(128)}) all-reduce(f32[]{:T(128)} %get-tuple-element.14, f32[]{:T(128)} %get-tuple-element.13), channel_id=1, replica_groups=mesh['gx'=4,'gy'=4,'gz'=2] {'gx','gy','gz'}, use_global_device_ids=true, to_apply=%region_1.2 | all-reduce | flops 2 | bytes 16 | tf_op jit(solution)/shard_map/psum | solution.py:151
  346.7 4.8 collective-permute-start.55
  379.5 5.1 collective-permute-start.61
  414.2 5.1 collective-permute-start.67
  438.3 4.7 collective-permute-start.72
  457.7 44.4 %all-reduce.1 = (f32[]{:T(128)}, f32[]{:T(128)}) all-reduce(f32[]{:T(128)} %get-tuple-element.9, f32[]{:T(128)} %get-tuple-element.8), channel_id=1, replica_groups=mesh['gx'=4,'gy'=4,'gz'=2] {'gx','gy','gz'}, use_global_device_ids=true, to_apply=%region_5.6 | all-reduce | flops 2 | bytes 16 | tf_op jit(solution)/shard_map/psum | solution.py:151
  516.8 4.8 collective-permute-start.79
  547.2 5.1 collective-permute-start.85
  553.6 4.5 collective-permute-start.87
  580.6 5.2 collective-permute-start.91
  587.0 4.5 collective-permute-start.93
  604.5 4.7 collective-permute-start.96
  619.3 40.5 %all-reduce = (f32[]{:T(128)}, f32[]{:T(128)}, f32[]{:T(128)}, f32[]{:T(128)}, f32[]{:T(128)}) all-reduce(f32[]{:T(128)} %get-tuple-element.7, f32[]{:T(128)} %get-tuple-element.12, f32[]{:T(128)} %get-tuple-element.6, f32[]{:T(128)} %get-tuple-element.10, f32[]{:T(128)} %get-tuple-element.11), channel_id=1, replica_groups=mesh['gx'=4,'gy'=4,'gz'=2] {'gx','gy','gz'}, use_global_device_ids=true, to_apply=%region_9.10 | all-reduce | flops 5 | bytes 40 | tf_op jit(solution)/shard_map/psum | solution.py:151
  (524 shorter events, 409.3 us)
Async XLA Ops:
  78.7 18.7 %collective-permute-start.17 = (f32[3,32,16,1]{1,2,3,0:T(8,128)}, f32[3,32,16,1]{1,2,3,0:T(8,128)}, u32[]{:S(2)}, u32[]{:S(2)}) collective-permute-start(f32[3,32,16,1]{1,2,3,0:T(8,128)} %copy.26), channel_id=1, source_target_pairs={{0,1},{2,3},{4,5},{6,7},{8,9},{10,11},{12,13},{14,15},{16,17},{18,... | collective-permute-start | bytes 18440 | tf_op jit(solution)/shard_map/ppermute | solution.py:14
  82.9 20.5 %collective-permute-start.13 = (f32[3,1,16,128]{3,2,1,0:T(8,128)}, f32[3,1,16,128]{3,2,1,0:T(8,128)}, u32[]{:S(2)}, u32[]{:S(2)}) collective-permute-start(f32[3,1,16,128]{3,2,1,0:T(8,128)} %get-tuple-element.172), channel_id=1, source_target_pairs={{0,8},{8,16},{16,24},{1,9},{9,17},{17,25},{2,10},{10,18},{18,26},{... | collective-permute-start | bytes 73736 | tf_op jit(solution)/shard_map/ppermute | solution.py:14
  114.4 17.8 %collective-permute-start.23 = (f32[3,32,16,1]{1,2,3,0:T(8,128)}, f32[3,32,16,1]{1,2,3,0:T(8,128)}, u32[]{:S(2)}, u32[]{:S(2)}) collective-permute-start(f32[3,32,16,1]{1,2,3,0:T(8,128)} %copy.30), channel_id=1, source_target_pairs={{0,1},{2,3},{4,5},{6,7},{8,9},{10,11},{12,13},{14,15},{16,17},{18,... | collective-permute-start | bytes 18440 | tf_op jit(solution)/shard_map/ppermute | solution.py:14
  118.6 20.3 %collective-permute-start.19 = (f32[3,1,16,128]{3,2,1,0:T(8,128)}, f32[3,1,16,128]{3,2,1,0:T(8,128)}, u32[]{:S(2)}, u32[]{:S(2)}) collective-permute-start(f32[3,1,16,128]{3,2,1,0:T(8,128)} %get-tuple-element.160), channel_id=1, source_target_pairs={{0,8},{8,16},{16,24},{1,9},{9,17},{17,25},{2,10},{10,18},{18,26},{... | collective-permute-start | bytes 73736 | tf_op jit(solution)/shard_map/ppermute | solution.py:14
  175.8 20.1 %collective-permute-start.31 = (f32[3,1,16,128]{3,2,1,0:T(8,128)}, f32[3,1,16,128]{3,2,1,0:T(8,128)}, u32[]{:S(2)}, u32[]{:S(2)}) collective-permute-start(f32[3,1,16,128]{3,2,1,0:T(8,128)} %get-tuple-element.146), channel_id=1, source_target_pairs={{0,8},{8,16},{16,24},{1,9},{9,17},{17,25},{2,10},{10,18},{18,26},{... | collective-permute-start | bytes 73736 | tf_op jit(solution)/shard_map/ppermute | solution.py:14
  206.7 18.1 %collective-permute-start.41 = (f32[3,32,16,1]{1,2,3,0:T(8,128)}, f32[3,32,16,1]{1,2,3,0:T(8,128)}, u32[]{:S(2)}, u32[]{:S(2)}) collective-permute-start(f32[3,32,16,1]{1,2,3,0:T(8,128)} %copy.38), channel_id=1, source_target_pairs={{0,1},{2,3},{4,5},{6,7},{8,9},{10,11},{12,13},{14,15},{16,17},{18,... | collective-permute-start | bytes 18440 | tf_op jit(solution)/shard_map/ppermute | solution.py:14
  211.6 19.4 %collective-permute-start.37 = (f32[3,1,16,128]{3,2,1,0:T(8,128)}, f32[3,1,16,128]{3,2,1,0:T(8,128)}, u32[]{:S(2)}, u32[]{:S(2)}) collective-permute-start(f32[3,1,16,128]{3,2,1,0:T(8,128)} %get-tuple-element.134), channel_id=1, source_target_pairs={{0,8},{8,16},{16,24},{1,9},{9,17},{17,25},{2,10},{10,18},{18,26},{... | collective-permute-start | bytes 73736 | tf_op jit(solution)/shard_map/ppermute | solution.py:14
  241.9 17.8 %collective-permute-start.47 = (f32[3,32,16,1]{1,2,3,0:T(8,128)}, f32[3,32,16,1]{1,2,3,0:T(8,128)}, u32[]{:S(2)}, u32[]{:S(2)}) collective-permute-start(f32[3,32,16,1]{1,2,3,0:T(8,128)} %copy.42), channel_id=1, source_target_pairs={{0,1},{2,3},{4,5},{6,7},{8,9},{10,11},{12,13},{14,15},{16,17},{18,... | collective-permute-start | bytes 18440 | tf_op jit(solution)/shard_map/ppermute | solution.py:14
  246.1 20.3 %collective-permute-start.43 = (f32[3,1,16,128]{3,2,1,0:T(8,128)}, f32[3,1,16,128]{3,2,1,0:T(8,128)}, u32[]{:S(2)}, u32[]{:S(2)}) collective-permute-start(f32[3,1,16,128]{3,2,1,0:T(8,128)} %get-tuple-element.122), channel_id=1, source_target_pairs={{0,8},{8,16},{16,24},{1,9},{9,17},{17,25},{2,10},{10,18},{18,26},{... | collective-permute-start | bytes 73736 | tf_op jit(solution)/shard_map/ppermute | solution.py:14
  286.0 50.4 %collective-permute-start.52 = (f32[32,1,128]{2,1,0:T(1,128)S(1)}, f32[32,1,128]{2,1,0:T(1,128)S(1)}, u32[]{:S(2)}, u32[]{:S(2)}) collective-permute-start(f32[32,1,128]{2,1,0:T(1,128)S(1)} %slice.1132), channel_id=1, source_target_pairs={{2,0},{4,2},{6,4},{3,1},{5,3},{7,5},{10,8},{12,10},{14,12},{11,9},... | collective-permute-start | bytes 49160 | tf_op jit(solution)/shard_map/ppermute | solution.py:14
  287.4 49.1 %collective-permute-start.51 = (f32[1,16,128]{2,1,0:T(8,128)S(1)}, f32[1,16,128]{2,1,0:T(8,128)S(1)}, u32[]{:S(2)}, u32[]{:S(2)}) collective-permute-start(f32[1,16,128]{2,1,0:T(8,128)S(1)} %slice.1130), channel_id=1, source_target_pairs={{8,0},{16,8},{24,16},{9,1},{17,9},{25,17},{10,2},{18,10},{26,18},{... | collective-permute-start | bytes 24584 | tf_op jit(solution)/shard_map/ppermute | solution.py:14
  288.7 47.8 %collective-permute-start.53 = (f32[32,16,1]{2,1,0:T(8,128)S(1)}, f32[32,16,1]{2,1,0:T(8,128)S(1)}, u32[]{:S(2)}, u32[]{:S(2)}) collective-permute-start(f32[32,16,1]{2,1,0:T(8,128)S(1)} %bitcast.173), channel_id=1, source_target_pairs={{1,0},{3,2},{5,4},{7,6},{9,8},{11,10},{13,12},{15,14},{17,16},{19,... | collective-permute-start | bytes 6152 | tf_op jit(solution)/shard_map/ppermute | solution.py:14
  346.7 17.2 %collective-permute-start.55 = (f32[3,1,16,128]{3,2,1,0:T(8,128)}, f32[3,1,16,128]{3,2,1,0:T(8,128)}, u32[]{:S(2)}, u32[]{:S(2)}) collective-permute-start(f32[3,1,16,128]{3,2,1,0:T(8,128)} %get-tuple-element.108), channel_id=1, source_target_pairs={{0,8},{8,16},{16,24},{1,9},{9,17},{17,25},{2,10},{10,18},{18,26},{... | collective-permute-start | bytes 73736 | tf_op jit(solution)/shard_map/ppermute | solution.py:14
  374.7 18.5 %collective-permute-start.65 = (f32[3,32,16,1]{1,2,3,0:T(8,128)}, f32[3,32,16,1]{1,2,3,0:T(8,128)}, u32[]{:S(2)}, u32[]{:S(2)}) collective-permute-start(f32[3,32,16,1]{1,2,3,0:T(8,128)} %copy.50), channel_id=1, source_target_pairs={{0,1},{2,3},{4,5},{6,7},{8,9},{10,11},{12,13},{14,15},{16,17},{18,... | collective-permute-start | bytes 18440 | tf_op jit(solution)/shard_map/ppermute | solution.py:14
  379.5 19.6 %collective-permute-start.61 = (f32[3,1,16,128]{3,2,1,0:T(8,128)}, f32[3,1,16,128]{3,2,1,0:T(8,128)}, u32[]{:S(2)}, u32[]{:S(2)}) collective-permute-start(f32[3,1,16,128]{3,2,1,0:T(8,128)} %get-tuple-element.96), channel_id=1, source_target_pairs={{0,8},{8,16},{16,24},{1,9},{9,17},{17,25},{2,10},{10,18},{18,26},{... | collective-permute-start | bytes 73736 | tf_op jit(solution)/shard_map/ppermute | solution.py:14
  410.0 17.5 %collective-permute-start.71 = (f32[3,32,16,1]{1,2,3,0:T(8,128)}, f32[3,32,16,1]{1,2,3,0:T(8,128)}, u32[]{:S(2)}, u32[]{:S(2)}) collective-permute-start(f32[3,32,16,1]{1,2,3,0:T(8,128)} %copy.54), channel_id=1, source_target_pairs={{0,1},{2,3},{4,5},{6,7},{8,9},{10,11},{12,13},{14,15},{16,17},{18,... | collective-permute-start | bytes 18440 | tf_op jit(solution)/shard_map/ppermute | solution.py:14
  414.2 20.0 %collective-permute-start.67 = (f32[3,1,16,128]{3,2,1,0:T(8,128)}, f32[3,1,16,128]{3,2,1,0:T(8,128)}, u32[]{:S(2)}, u32[]{:S(2)}) collective-permute-start(f32[3,1,16,128]{3,2,1,0:T(8,128)} %get-tuple-element.84), channel_id=1, source_target_pairs={{0,8},{8,16},{16,24},{1,9},{9,17},{17,25},{2,10},{10,18},{18,26},{... | collective-permute-start | bytes 73736 | tf_op jit(solution)/shard_map/ppermute | solution.py:14
  453.8 52.8 %collective-permute-start.76 = (f32[32,1,128]{2,1,0:T(1,128)S(1)}, f32[32,1,128]{2,1,0:T(1,128)S(1)}, u32[]{:S(2)}, u32[]{:S(2)}) collective-permute-start(f32[32,1,128]{2,1,0:T(1,128)S(1)} %slice.1183), channel_id=1, source_target_pairs={{2,0},{4,2},{6,4},{3,1},{5,3},{7,5},{10,8},{12,10},{14,12},{11,9},... | collective-permute-start | bytes 49160 | tf_op jit(solution)/shard_map/ppermute | solution.py:14
  455.1 51.5 %collective-permute-start.75 = (f32[1,16,128]{2,1,0:T(8,128)S(1)}, f32[1,16,128]{2,1,0:T(8,128)S(1)}, u32[]{:S(2)}, u32[]{:S(2)}) collective-permute-start(f32[1,16,128]{2,1,0:T(8,128)S(1)} %slice.1181), channel_id=1, source_target_pairs={{8,0},{16,8},{24,16},{9,1},{17,9},{25,17},{10,2},{18,10},{26,18},{... | collective-permute-start | bytes 24584 | tf_op jit(solution)/shard_map/ppermute | solution.py:14
  456.4 50.2 %collective-permute-start.77 = (f32[32,16,1]{2,1,0:T(8,128)S(1)}, f32[32,16,1]{2,1,0:T(8,128)S(1)}, u32[]{:S(2)}, u32[]{:S(2)}) collective-permute-start(f32[32,16,1]{2,1,0:T(8,128)S(1)} %bitcast.174), channel_id=1, source_target_pairs={{1,0},{3,2},{5,4},{7,6},{9,8},{11,10},{13,12},{15,14},{17,16},{19,... | collective-permute-start | bytes 6152 | tf_op jit(solution)/shard_map/ppermute | solution.py:14
  516.8 18.2 %collective-permute-start.79 = (f32[3,1,16,128]{3,2,1,0:T(8,128)}, f32[3,1,16,128]{3,2,1,0:T(8,128)}, u32[]{:S(2)}, u32[]{:S(2)}) collective-permute-start(f32[3,1,16,128]{3,2,1,0:T(8,128)} %get-tuple-element.70), channel_id=1, source_target_pairs={{0,8},{8,16},{16,24},{1,9},{9,17},{17,25},{2,10},{10,18},{18,26},{... | collective-permute-start | bytes 73736 | tf_op jit(solution)/shard_map/ppermute | solution.py:14
  547.2 18.4 %collective-permute-start.85 = (f32[3,1,16,128]{3,2,1,0:T(8,128)}, f32[3,1,16,128]{3,2,1,0:T(8,128)}, u32[]{:S(2)}, u32[]{:S(2)}) collective-permute-start(f32[3,1,16,128]{3,2,1,0:T(8,128)} %get-tuple-element.58), channel_id=1, source_target_pairs={{0,8},{8,16},{16,24},{1,9},{9,17},{17,25},{2,10},{10,18},{18,26},{... | collective-permute-start | bytes 73736 | tf_op jit(solution)/shard_map/ppermute | solution.py:14
  576.3 17.5 %collective-permute-start.95 = (f32[3,32,16,1]{1,2,3,0:T(8,128)}, f32[3,32,16,1]{1,2,3,0:T(8,128)}, u32[]{:S(2)}, u32[]{:S(2)}) collective-permute-start(f32[3,32,16,1]{1,2,3,0:T(8,128)} %copy.66), channel_id=1, source_target_pairs={{0,1},{2,3},{4,5},{6,7},{8,9},{10,11},{12,13},{14,15},{16,17},{18,... | collective-permute-start | bytes 18440 | tf_op jit(solution)/shard_map/ppermute | solution.py:14
  580.6 20.0 %collective-permute-start.91 = (f32[3,1,16,128]{3,2,1,0:T(8,128)}, f32[3,1,16,128]{3,2,1,0:T(8,128)}, u32[]{:S(2)}, u32[]{:S(2)}) collective-permute-start(f32[3,1,16,128]{3,2,1,0:T(8,128)} %get-tuple-element.46), channel_id=1, source_target_pairs={{0,8},{8,16},{16,24},{1,9},{9,17},{17,25},{2,10},{10,18},{18,26},{... | collective-permute-start | bytes 73736 | tf_op jit(solution)/shard_map/ppermute | solution.py:14
  (147 other events, 1214.1 us)
where the time goes:
time: 679 us; the launch traced here: 667 us
  starting transfers between devices  274 us (40%)
  local copies, waits for them, and re-layouts  165 us (24%)
  blocking collectives  130 us (19%)
  other arithmetic  64.1 us (9%)
  between operations  21.6 us (3%)
  waiting for transfers between devices  12.4 us (2%)
    ppermute x93, starting transfers between devices, passed_along(): return lax.ppermute(value, axis, pairs)  259 us
    psum x3, blocking collectives, per_device(): lax.psum((jnp.sum(residual * scaled), jnp.sum(applied * scaled), jnp.sum(...  130 us
    slice x48, local copies, waits for them, and re-layouts, viscous(): tail = lax.slice_in_dim(state, length - 1, length, axis=dim)  52.2 us
    add x12, other arithmetic, sweeps(): state = state + OMEGA * inverse * (source - viscous(state, faces, diag))  48.6 us
    slice x36, local copies, waits for them, and re-layouts, viscous(): lax.slice_in_dim(state, 0, length - 1, axis=dim)  48.5 us
    ppermute x24, local copies, waits for them, and re-layouts, passed_along(): return lax.ppermute(value, axis, pairs)  42.5 us
  transfers between devices with their start and end apart: 99, of which 8 were waited for; matrix products, arithmetic and copies ran while one was open for 12% of the time, Pallas kernels for 0%

commit v1 on v0

--- a/solution.py
+++ b/solution.py
@@ -149,8 +149,15 @@
     for step in range(ITERS):
         last = step + 1 == ITERS
         gamma, delta, squares = lax.psum(
-            (jnp.sum(residual * scaled), jnp.sum(applied * scaled), jnp.sum(residual * residual)),
-            ("gx", "gy", "gz"),
+            lax.psum(
+                (
+                    jnp.sum(residual * scaled),
+                    jnp.sum(applied * scaled),
+                    jnp.sum(residual * residual),
+                ),
+                ("gy", "gz"),
+            ),
+            "gx",
         )
         norms.append(squares / cells)
         if not last:

time: 679 us -> 626 us (0.922)
  blocking collectives: 130 us -> 84.1 us
    psum x3, blocking collectives: 130 us -> 49.8 us  [per_device(): lax.psum((jnp.sum(residual * scaled), jnp.sum(applied * scaled), jnp.sum(...]
    psum x0 -> x3, blocking collectives: none -> 34.2 us  [per_device(): lax.psum(lax.psum((jnp.sum(residual * scaled), jnp.sum(applied * scaled),...]
  transfers between devices with their start and end apart: 99 -> 99, of which waited for: 8 -> 8; matrix products, arithmetic and copies ran while one was open for 12% -> 13% of each run, Pallas kernels for 0% -> 0%
where the time goes in v1:
time: 626 us; the launch traced here: 615 us
  starting transfers between devices  268 us (43%)
  local copies, waits for them, and re-layouts  164 us (26%)
  blocking collectives  84.1 us (13%)
  other arithmetic  64.2 us (10%)
  between operations  22 us (4%)
  waiting for transfers between devices  12.4 us (2%)
    ppermute x93, starting transfers between devices, passed_along(): return lax.ppermute(value, axis, pairs)  253 us
    slice x48, local copies, waits for them, and re-layouts, viscous(): tail = lax.slice_in_dim(state, length - 1, length, axis=dim)  51.9 us
    psum x3, blocking collectives, per_device(): lax.psum((jnp.sum(residual * scaled), jnp.sum(applied * scaled), jnp.sum(...  49.8 us
    slice x36, local copies, waits for them, and re-layouts, viscous(): lax.slice_in_dim(state, 0, length - 1, axis=dim)  48.7 us
    add x12, other arithmetic, sweeps(): state = state + OMEGA * inverse * (source - viscous(state, faces, diag))  48.5 us
    ppermute x24, local copies, waits for them, and re-layouts, passed_along(): return lax.ppermute(value, axis, pairs)  41.7 us
    psum x3, blocking collectives, per_device(): lax.psum(lax.psum((jnp.sum(residual * scaled), jnp.sum(applied * scaled),...  34.2 us
  transfers between devices with their start and end apart: 99, of which 8 were waited for; matrix products, arithmetic and copies ran while one was open for 13% of the time, Pallas kernels for 0%

profile of v1, /device:TPU:0, one launch (start us, length us, event | category | flops | bytes accessed | tf_op | source)
XLA Modules:
  0.0 614.6 jit_solution(1503515150353310363)
XLA Ops:
  2.6 5.5 collective-permute-start
  31.0 6.0 select_add_fusion
  82.9 6.3 %collective-permute-start.13 = (f32[3,1,16,128]{3,2,1,0:T(8,128)}, f32[3,1,16,128]{3,2,1,0:T(8,128)}, u32[]{:S(2)}, u32[]{:S(2)}) collective-permute-start(f32[3,1,16,128]{3,2,1,0:T(8,128)} %get-tuple-element.181), channel_id=1, source_target_pairs={{0,8},{8,16},{16,24},{1,9},{9,17},{17,25},{2,10},{10,18},{18,26},{... | collective-permute-start | bytes 73736 | tf_op jit(solution)/shard_map/ppermute | solution.py:14
  118.5 5.5 collective-permute-start.19
  142.9 4.9 collective-permute-start.24
  175.8 5.3 collective-permute-start.31
  182.4 4.5 collective-permute-start.33
  211.6 5.1 collective-permute-start.37
  246.2 5.5 collective-permute-start.43
  270.5 4.9 collective-permute-start.48
  290.1 18.4 %all-reduce.2 = (f32[]{:T(128)}, f32[]{:T(128)}) all-reduce(f32[]{:T(128)} %get-tuple-element.14, f32[]{:T(128)} %get-tuple-element.13), channel_id=1, replica_groups=mesh['gx'=4,'gy'=4,'gz'=2] {'gy','gz'}, use_global_device_ids=true, to_apply=%region_1.2 | all-reduce | flops 2 | bytes 16 | tf_op jit(solution)/shard_map/psum | solution.py:152
  308.5 12.0 %all-reduce.5 = (f32[]{:T(128)}, f32[]{:T(128)}) all-reduce(f32[]{:T(128)} %get-tuple-element.22, f32[]{:T(128)} %get-tuple-element.23), channel_id=1, replica_groups=mesh['gx'=4,'gy'=4,'gz'=2] {'gx'}, use_global_device_ids=true, to_apply=%region_2.3 | all-reduce | flops 2 | bytes 16 | tf_op jit(solution)/shard_map/psum | solution.py:151
  363.7 5.1 collective-permute-start.61
  398.5 5.1 collective-permute-start.67
  422.5 4.7 collective-permute-start.72
  442.0 16.7 %all-reduce.1 = (f32[]{:T(128)}, f32[]{:T(128)}) all-reduce(f32[]{:T(128)} %get-tuple-element.9, f32[]{:T(128)} %get-tuple-element.8), channel_id=1, replica_groups=mesh['gx'=4,'gy'=4,'gz'=2] {'gy','gz'}, use_global_device_ids=true, to_apply=%region_7.8 | all-reduce | flops 2 | bytes 16 | tf_op jit(solution)/shard_map/psum | solution.py:152
  458.7 11.6 %all-reduce.4 = (f32[]{:T(128)}, f32[]{:T(128)}) all-reduce(f32[]{:T(128)} %get-tuple-element.20, f32[]{:T(128)} %get-tuple-element.21), channel_id=1, replica_groups=mesh['gx'=4,'gy'=4,'gz'=2] {'gx'}, use_global_device_ids=true, to_apply=%region_8.9 | all-reduce | flops 2 | bytes 16 | tf_op jit(solution)/shard_map/psum | solution.py:151
  510.6 4.5 collective-permute-start.85
  516.4 4.5 collective-permute-start.87
  543.0 5.1 collective-permute-start.91
  549.4 4.5 collective-permute-start.93
  566.9 4.7 collective-permute-start.96
  581.7 14.7 %all-reduce = (f32[]{:T(128)}, f32[]{:T(128)}, f32[]{:T(128)}, f32[]{:T(128)}, f32[]{:T(128)}) all-reduce(f32[]{:T(128)} %get-tuple-element.7, f32[]{:T(128)} %get-tuple-element.12, f32[]{:T(128)} %get-tuple-element.6, f32[]{:T(128)} %get-tuple-element.10, f32[]{:T(128)} %get-tuple-element.11), channel_id=1, replica_groups=mesh['gx'=4,'gy'=4,'gz'=2] {'gy','gz'}, use_global_device_ids=true, to_apply=%region_13.14 | all-reduce | flops 5 | bytes 40 | tf_op jit(solution)/shard_map/psum | solution.py:152
  596.3 10.6 %all-reduce.3 = (f32[]{:T(128)}, f32[]{:T(128)}, f32[]{:T(128)}, f32[]{:T(128)}, f32[]{:T(128)}) all-reduce(f32[]{:T(128)} %get-tuple-element.15, f32[]{:T(128)} %get-tuple-element.16, f32[]{:T(128)} %get-tuple-element.17, f32[]{:T(128)} %get-tuple-element.18, f32[]{:T(128)} %get-tuple-element.19), channel_id=1, replica_groups=mesh['gx'=4,'gy'=4,'gz'=2] {'gx'}, use_global_device_ids=true, to_apply=%region_14.15 | all-reduce | flops 5 | bytes 40 | tf_op jit(solution)/shard_map/psum | solution.py:151
  (527 shorter events, 416.7 us)
Async XLA Ops:
  50.6 16.7 %collective-permute-start.7 = (f32[3,1,16,128]{3,2,1,0:T(8,128)}, f32[3,1,16,128]{3,2,1,0:T(8,128)S(1)}, u32[]{:S(2)}, u32[]{:S(2)}) collective-permute-start(f32[3,1,16,128]{3,2,1,0:T(8,128)} %get-tuple-element.193), channel_id=1, source_target_pairs={{0,8},{8,16},{16,24},{1,9},{9,17},{17,25},{2,10},{10,18},{18,26},{... | collective-permute-start | bytes 73736 | tf_op jit(solution)/shard_map/ppermute | solution.py:14
  78.6 18.7 %collective-permute-start.17 = (f32[3,32,16,1]{1,2,3,0:T(8,128)}, f32[3,32,16,1]{1,2,3,0:T(8,128)}, u32[]{:S(2)}, u32[]{:S(2)}) collective-permute-start(f32[3,32,16,1]{1,2,3,0:T(8,128)} %copy.26), channel_id=1, source_target_pairs={{0,1},{2,3},{4,5},{6,7},{8,9},{10,11},{12,13},{14,15},{16,17},{18,... | collective-permute-start | bytes 18440 | tf_op jit(solution)/shard_map/ppermute | solution.py:14
  82.9 20.5 %collective-permute-start.13 = (f32[3,1,16,128]{3,2,1,0:T(8,128)}, f32[3,1,16,128]{3,2,1,0:T(8,128)}, u32[]{:S(2)}, u32[]{:S(2)}) collective-permute-start(f32[3,1,16,128]{3,2,1,0:T(8,128)} %get-tuple-element.181), channel_id=1, source_target_pairs={{0,8},{8,16},{16,24},{1,9},{9,17},{17,25},{2,10},{10,18},{18,26},{... | collective-permute-start | bytes 73736 | tf_op jit(solution)/shard_map/ppermute | solution.py:14
  114.3 17.8 %collective-permute-start.23 = (f32[3,32,16,1]{1,2,3,0:T(8,128)}, f32[3,32,16,1]{1,2,3,0:T(8,128)}, u32[]{:S(2)}, u32[]{:S(2)}) collective-permute-start(f32[3,32,16,1]{1,2,3,0:T(8,128)} %copy.30), channel_id=1, source_target_pairs={{0,1},{2,3},{4,5},{6,7},{8,9},{10,11},{12,13},{14,15},{16,17},{18,... | collective-permute-start | bytes 18440 | tf_op jit(solution)/shard_map/ppermute | solution.py:14
  118.5 20.3 %collective-permute-start.19 = (f32[3,1,16,128]{3,2,1,0:T(8,128)}, f32[3,1,16,128]{3,2,1,0:T(8,128)}, u32[]{:S(2)}, u32[]{:S(2)}) collective-permute-start(f32[3,1,16,128]{3,2,1,0:T(8,128)} %get-tuple-element.169), channel_id=1, source_target_pairs={{0,8},{8,16},{16,24},{1,9},{9,17},{17,25},{2,10},{10,18},{18,26},{... | collective-permute-start | bytes 73736 | tf_op jit(solution)/shard_map/ppermute | solution.py:14
  173.2 16.0 %collective-permute-start.35 = (f32[3,32,16,1]{1,2,3,0:T(8,128)}, f32[3,32,16,1]{1,2,3,0:T(8,128)}, u32[]{:S(2)}, u32[]{:S(2)}) collective-permute-start(f32[3,32,16,1]{1,2,3,0:T(8,128)} %copy.34), channel_id=1, source_target_pairs={{0,1},{2,3},{4,5},{6,7},{8,9},{10,11},{12,13},{14,15},{16,17},{18,... | collective-permute-start | bytes 18440 | tf_op jit(solution)/shard_map/ppermute | solution.py:14
  175.8 20.1 %collective-permute-start.31 = (f32[3,1,16,128]{3,2,1,0:T(8,128)}, f32[3,1,16,128]{3,2,1,0:T(8,128)}, u32[]{:S(2)}, u32[]{:S(2)}) collective-permute-start(f32[3,1,16,128]{3,2,1,0:T(8,128)} %get-tuple-element.155), channel_id=1, source_target_pairs={{0,8},{8,16},{16,24},{1,9},{9,17},{17,25},{2,10},{10,18},{18,26},{... | collective-permute-start | bytes 73736 | tf_op jit(solution)/shard_map/ppermute | solution.py:14
  206.8 18.1 %collective-permute-start.41 = (f32[3,32,16,1]{1,2,3,0:T(8,128)}, f32[3,32,16,1]{1,2,3,0:T(8,128)}, u32[]{:S(2)}, u32[]{:S(2)}) collective-permute-start(f32[3,32,16,1]{1,2,3,0:T(8,128)} %copy.38), channel_id=1, source_target_pairs={{0,1},{2,3},{4,5},{6,7},{8,9},{10,11},{12,13},{14,15},{16,17},{18,... | collective-permute-start | bytes 18440 | tf_op jit(solution)/shard_map/ppermute | solution.py:14
  211.6 19.4 %collective-permute-start.37 = (f32[3,1,16,128]{3,2,1,0:T(8,128)}, f32[3,1,16,128]{3,2,1,0:T(8,128)}, u32[]{:S(2)}, u32[]{:S(2)}) collective-permute-start(f32[3,1,16,128]{3,2,1,0:T(8,128)} %get-tuple-element.143), channel_id=1, source_target_pairs={{0,8},{8,16},{16,24},{1,9},{9,17},{17,25},{2,10},{10,18},{18,26},{... | collective-permute-start | bytes 73736 | tf_op jit(solution)/shard_map/ppermute | solution.py:14
  241.9 17.8 %collective-permute-start.47 = (f32[3,32,16,1]{1,2,3,0:T(8,128)}, f32[3,32,16,1]{1,2,3,0:T(8,128)}, u32[]{:S(2)}, u32[]{:S(2)}) collective-permute-start(f32[3,32,16,1]{1,2,3,0:T(8,128)} %copy.42), channel_id=1, source_target_pairs={{0,1},{2,3},{4,5},{6,7},{8,9},{10,11},{12,13},{14,15},{16,17},{18,... | collective-permute-start | bytes 18440 | tf_op jit(solution)/shard_map/ppermute | solution.py:14
  246.2 20.3 %collective-permute-start.43 = (f32[3,1,16,128]{3,2,1,0:T(8,128)}, f32[3,1,16,128]{3,2,1,0:T(8,128)}, u32[]{:S(2)}, u32[]{:S(2)}) collective-permute-start(f32[3,1,16,128]{3,2,1,0:T(8,128)} %get-tuple-element.131), channel_id=1, source_target_pairs={{0,8},{8,16},{16,24},{1,9},{9,17},{17,25},{2,10},{10,18},{18,26},{... | collective-permute-start | bytes 73736 | tf_op jit(solution)/shard_map/ppermute | solution.py:14
  286.1 35.9 %collective-permute-start.52 = (f32[32,1,128]{2,1,0:T(1,128)S(1)}, f32[32,1,128]{2,1,0:T(1,128)S(1)}, u32[]{:S(2)}, u32[]{:S(2)}) collective-permute-start(f32[32,1,128]{2,1,0:T(1,128)S(1)} %slice.1132), channel_id=1, source_target_pairs={{2,0},{4,2},{6,4},{3,1},{5,3},{7,5},{10,8},{12,10},{14,12},{11,9},... | collective-permute-start | bytes 49160 | tf_op jit(solution)/shard_map/ppermute | solution.py:14
  287.5 34.6 %collective-permute-start.51 = (f32[1,16,128]{2,1,0:T(8,128)S(1)}, f32[1,16,128]{2,1,0:T(8,128)S(1)}, u32[]{:S(2)}, u32[]{:S(2)}) collective-permute-start(f32[1,16,128]{2,1,0:T(8,128)S(1)} %slice.1130), channel_id=1, source_target_pairs={{8,0},{16,8},{24,16},{9,1},{17,9},{25,17},{10,2},{18,10},{26,18},{... | collective-permute-start | bytes 24584 | tf_op jit(solution)/shard_map/ppermute | solution.py:14
  288.8 33.3 %collective-permute-start.53 = (f32[32,16,1]{2,1,0:T(8,128)S(1)}, f32[32,16,1]{2,1,0:T(8,128)S(1)}, u32[]{:S(2)}, u32[]{:S(2)}) collective-permute-start(f32[32,16,1]{2,1,0:T(8,128)S(1)} %bitcast.173), channel_id=1, source_target_pairs={{1,0},{3,2},{5,4},{7,6},{9,8},{11,10},{13,12},{15,14},{17,16},{19,... | collective-permute-start | bytes 6152 | tf_op jit(solution)/shard_map/ppermute | solution.py:14
  358.9 18.1 %collective-permute-start.65 = (f32[3,32,16,1]{1,2,3,0:T(8,128)}, f32[3,32,16,1]{1,2,3,0:T(8,128)}, u32[]{:S(2)}, u32[]{:S(2)}) collective-permute-start(f32[3,32,16,1]{1,2,3,0:T(8,128)} %copy.50), channel_id=1, source_target_pairs={{0,1},{2,3},{4,5},{6,7},{8,9},{10,11},{12,13},{14,15},{16,17},{18,... | collective-permute-start | bytes 18440 | tf_op jit(solution)/shard_map/ppermute | solution.py:14
  363.7 19.5 %collective-permute-start.61 = (f32[3,1,16,128]{3,2,1,0:T(8,128)}, f32[3,1,16,128]{3,2,1,0:T(8,128)}, u32[]{:S(2)}, u32[]{:S(2)}) collective-permute-start(f32[3,1,16,128]{3,2,1,0:T(8,128)} %get-tuple-element.105), channel_id=1, source_target_pairs={{0,8},{8,16},{16,24},{1,9},{9,17},{17,25},{2,10},{10,18},{18,26},{... | collective-permute-start | bytes 73736 | tf_op jit(solution)/shard_map/ppermute | solution.py:14
  394.2 17.5 %collective-permute-start.71 = (f32[3,32,16,1]{1,2,3,0:T(8,128)}, f32[3,32,16,1]{1,2,3,0:T(8,128)}, u32[]{:S(2)}, u32[]{:S(2)}) collective-permute-start(f32[3,32,16,1]{1,2,3,0:T(8,128)} %copy.54), channel_id=1, source_target_pairs={{0,1},{2,3},{4,5},{6,7},{8,9},{10,11},{12,13},{14,15},{16,17},{18,... | collective-permute-start | bytes 18440 | tf_op jit(solution)/shard_map/ppermute | solution.py:14
  398.5 20.0 %collective-permute-start.67 = (f32[3,1,16,128]{3,2,1,0:T(8,128)}, f32[3,1,16,128]{3,2,1,0:T(8,128)}, u32[]{:S(2)}, u32[]{:S(2)}) collective-permute-start(f32[3,1,16,128]{3,2,1,0:T(8,128)} %get-tuple-element.93), channel_id=1, source_target_pairs={{0,8},{8,16},{16,24},{1,9},{9,17},{17,25},{2,10},{10,18},{18,26},{... | collective-permute-start | bytes 73736 | tf_op jit(solution)/shard_map/ppermute | solution.py:14
  438.0 37.1 %collective-permute-start.76 = (f32[32,1,128]{2,1,0:T(1,128)S(1)}, f32[32,1,128]{2,1,0:T(1,128)S(1)}, u32[]{:S(2)}, u32[]{:S(2)}) collective-permute-start(f32[32,1,128]{2,1,0:T(1,128)S(1)} %slice.1183), channel_id=1, source_target_pairs={{2,0},{4,2},{6,4},{3,1},{5,3},{7,5},{10,8},{12,10},{14,12},{11,9},... | collective-permute-start | bytes 49160 | tf_op jit(solution)/shard_map/ppermute | solution.py:14
  439.4 35.8 %collective-permute-start.75 = (f32[1,16,128]{2,1,0:T(8,128)S(1)}, f32[1,16,128]{2,1,0:T(8,128)S(1)}, u32[]{:S(2)}, u32[]{:S(2)}) collective-permute-start(f32[1,16,128]{2,1,0:T(8,128)S(1)} %slice.1181), channel_id=1, source_target_pairs={{8,0},{16,8},{24,16},{9,1},{17,9},{25,17},{10,2},{18,10},{26,18},{... | collective-permute-start | bytes 24584 | tf_op jit(solution)/shard_map/ppermute | solution.py:14
  440.7 34.5 %collective-permute-start.77 = (f32[32,16,1]{2,1,0:T(8,128)S(1)}, f32[32,16,1]{2,1,0:T(8,128)S(1)}, u32[]{:S(2)}, u32[]{:S(2)}) collective-permute-start(f32[32,16,1]{2,1,0:T(8,128)S(1)} %bitcast.174), channel_id=1, source_target_pairs={{1,0},{3,2},{5,4},{7,6},{9,8},{11,10},{13,12},{15,14},{17,16},{19,... | collective-permute-start | bytes 6152 | tf_op jit(solution)/shard_map/ppermute | solution.py:14
  510.6 17.4 %collective-permute-start.85 = (f32[3,1,16,128]{3,2,1,0:T(8,128)S(1)}, f32[3,1,16,128]{3,2,1,0:T(8,128)S(1)}, u32[]{:S(2)}, u32[]{:S(2)}) collective-permute-start(f32[3,1,16,128]{3,2,1,0:T(8,128)S(1)} %get-tuple-element.67), channel_id=1, source_target_pairs={{0,8},{8,16},{16,24},{1,9},{9,17},{17,25},{2,10},{10,18},{18,26},{... | collective-permute-start | bytes 73736 | tf_op jit(solution)/shard_map/ppermute | solution.py:14
  538.7 17.5 %collective-permute-start.95 = (f32[3,32,16,1]{1,2,3,0:T(8,128)}, f32[3,32,16,1]{1,2,3,0:T(8,128)}, u32[]{:S(2)}, u32[]{:S(2)}) collective-permute-start(f32[3,32,16,1]{1,2,3,0:T(8,128)} %copy.66), channel_id=1, source_target_pairs={{0,1},{2,3},{4,5},{6,7},{8,9},{10,11},{12,13},{14,15},{16,17},{18,... | collective-permute-start | bytes 18440 | tf_op jit(solution)/shard_map/ppermute | solution.py:14
  543.0 20.0 %collective-permute-start.91 = (f32[3,1,16,128]{3,2,1,0:T(8,128)}, f32[3,1,16,128]{3,2,1,0:T(8,128)}, u32[]{:S(2)}, u32[]{:S(2)}) collective-permute-start(f32[3,1,16,128]{3,2,1,0:T(8,128)} %get-tuple-element.55), channel_id=1, source_target_pairs={{0,8},{8,16},{16,24},{1,9},{9,17},{17,25},{2,10},{10,18},{18,26},{... | collective-permute-start | bytes 73736 | tf_op jit(solution)/shard_map/ppermute | solution.py:14
  (147 other events, 1163.7 us)
